TPU v7x, 32 devices: a whole 2x2x4 slice. The times are simulated.
32 devices in a mesh: dp: 8 (over z, x), tensor: 4 (over y, core).
Axes of the slice: x: 2, y: 2, z: 4, core: 2. Of those that a mesh axis runs over, the one named last changes fastest.
Arguments:
- tokens: bfloat16 [128, 64, 768], P('dp'), may hold values from -6 to 6
- image_tokens: bfloat16 [128, 256, 768], P('dp', None, 'tensor'), may hold values from -6 to 6
- image_counts: int32 [128], P('dp'), may hold values from 64 to 256, as said below
- ln1_gain: float32 [768], replicated, may hold values from 0.25 to 1.75
- ln1_bias: float32 [768], replicated, may hold values from -2 to 2
- self_qkv: bfloat16 [768, 3, 768], P(None, None, 'tensor'), may hold values from -0.21875 to 0.21875
- self_output_weight: bfloat16 [768, 768], P('tensor'), may hold values from -0.625 to 0.625
- self_output_bias: float32 [768], replicated, may hold values from -2 to 2
- ln2_gain: float32 [768], replicated, may hold values from 0.25 to 1.75
- ln2_bias: float32 [768], replicated, may hold values from -2 to 2
- cross_query_weight: bfloat16 [768, 768], P(None, 'tensor'), may hold values from -0.21875 to 0.21875
- cross_kv: bfloat16 [768, 2, 768], P(None, None, 'tensor'), may hold values from -0.21875 to 0.21875
- cross_output_weight: bfloat16 [768, 768], P('tensor'), may hold values from -0.625 to 0.625
- cross_output_bias: float32 [768], replicated, may hold values from -2 to 2
- ln3_gain: float32 [768], replicated, may hold values from 0.25 to 1.75
- ln3_bias: float32 [768], replicated, may hold values from -2 to 2
- mlp_in: bfloat16 [768, 3072], P(None, 'tensor'), may hold values from -0.21875 to 0.21875
- mlp_in_bias: float32 [3072], P('tensor'), may hold values from -3 to 3
- mlp_out: bfloat16 [3072, 768], P('tensor'), may hold values from -0.15625 to 0.15625
- mlp_out_bias: float32 [768], replicated, may hold values from -2 to 2
- grad_out: bfloat16 [128, 64, 768], P('dp'), may hold values from -6 to 6
Outputs:
- output: bfloat16 [128, 64, 768], P('dp')
- grad_tokens: bfloat16 [128, 64, 768], P('dp')
- grad_image: bfloat16 [128, 256, 768], P('dp', None, 'tensor')
- grad_ln1_gain: float32 [768], replicated
- grad_ln1_bias: float32 [768], replicated
- grad_self_qkv: float32 [768, 3, 768], P('dp', None, 'tensor')
- grad_self_out: float32 [768, 768], P('tensor', 'dp')
- grad_self_out_bias: float32 [768], replicated
- grad_ln2_gain: float32 [768], replicated
- grad_ln2_bias: float32 [768], replicated
- grad_cross_q: float32 [768, 768], P('dp', 'tensor')
- grad_cross_kv: float32 [768, 2, 768], P('dp', None, 'tensor')
- grad_cross_out: float32 [768, 768], P('tensor', 'dp')
- grad_cross_out_bias: float32 [768], replicated
- grad_ln3_gain: float32 [768], replicated
- grad_ln3_bias: float32 [768], replicated
- grad_mlp_in: float32 [768, 3072], P('dp', 'tensor')
- grad_mlp_in_bias: float32 [3072], P('tensor')
- grad_mlp_out: float32 [3072, 768], P('tensor', 'dp')
- grad_mlp_out_bias: float32 [768], replicated
Inputs may be any that keep to these rules, and one draw needn't show every extreme that they name: image_counts[c] is the number of leading image tokens that caption c attends to; both bounds are reached in every draw.
All inputs are finite; a program needn't handle non-finite values.
Results may differ from a plain program's by a relative error of at most 0.034.
Values may be sent and summed in bfloat16 or wider, within the bound.
A program may use at most 192 MiB of HBM per device.

v0:
```python
from functools import partial
import jax
import jax.numpy as jnp
from jax import lax
from jax.sharding import PartitionSpec as P

HEAD_SIZE = 64


def norm_parts(values):
    center = values - jnp.mean(values, axis=-1, keepdims=True)
    inv_std = lax.rsqrt(jnp.mean(center * center, axis=-1, keepdims=True) + 1e-05)
    return (center * inv_std, inv_std)


def norm_back(gradient, normed, inv_std, gain_row):
    scaled = gradient * gain_row
    return inv_std * (
        scaled
        - jnp.mean(scaled, axis=-1, keepdims=True)
        - normed * jnp.mean(scaled * normed, axis=-1, keepdims=True)
    )


def branch_total(term_rows):
    return lax.psum(term_rows.astype(jnp.bfloat16), "tensor").astype(jnp.float32)


def input_total(term_rows):
    return lax.psum(term_rows.astype(jnp.bfloat16), "tensor").astype(jnp.float32)


def attend_forward(queries, key_rows, value_rows, allowed, scaling):
    scores = (
        jnp.einsum("clhe,cmhe->chlm", queries, key_rows, preferred_element_type=jnp.float32)
        * scaling
    )
    scores = jnp.where(allowed[:, None], scores, -1000000000.0)
    highest = jnp.max(scores, axis=-1, keepdims=True)
    exponent = jnp.exp(scores - highest)
    chances = exponent / jnp.sum(exponent, axis=-1, keepdims=True)
    mixture = jnp.einsum(
        "chlm,cmhe->clhe",
        chances.astype(jnp.bfloat16),
        value_rows,
        preferred_element_type=jnp.float32,
    )
    return (mixture.astype(jnp.bfloat16), chances)


def attend_back(grad_mixture, queries, key_rows, value_rows, chances, scaling):
    grad_chances = jnp.einsum(
        "clhe,cmhe->chlm", grad_mixture, value_rows, preferred_element_type=jnp.float32
    )
    grad_values = jnp.einsum(
        "chlm,clhe->cmhe",
        chances.astype(jnp.bfloat16),
        grad_mixture,
        preferred_element_type=jnp.float32,
    )
    inner_sum = jnp.sum(grad_chances * chances, axis=-1, keepdims=True)
    grad_scores = (chances * (grad_chances - inner_sum)).astype(jnp.bfloat16)
    grad_queries = (
        jnp.einsum("chlm,cmhe->clhe", grad_scores, key_rows, preferred_element_type=jnp.float32)
        * scaling
    )
    grad_keys = (
        jnp.einsum("chlm,clhe->cmhe", grad_scores, queries, preferred_element_type=jnp.float32)
        * scaling
    )
    return (
        grad_queries.astype(jnp.bfloat16),
        grad_keys.astype(jnp.bfloat16),
        grad_values.astype(jnp.bfloat16),
    )


def local(
    tokens,
    image_tokens,
    image_counts,
    ln1_gain,
    ln1_bias,
    self_qkv,
    self_output_weight,
    self_output_bias,
    ln2_gain,
    ln2_bias,
    cross_query_weight,
    cross_kv,
    cross_output_weight,
    cross_output_bias,
    ln3_gain,
    ln3_bias,
    mlp_in,
    mlp_in_bias,
    mlp_out,
    mlp_out_bias,
    grad_out,
):
    captions, length, model_width = tokens.shape
    row_count = captions * length
    local_width = self_output_weight.shape[0]
    local_heads = local_width // HEAD_SIZE
    scaling = HEAD_SIZE ** (-0.5)
    residual = tokens.astype(jnp.float32).reshape(row_count, model_width)
    normed_one, inv_one = norm_parts(residual)
    in_one = (normed_one * ln1_gain + ln1_bias).astype(jnp.bfloat16)
    qkv_rows = jnp.einsum(
        "rd,dtk->rtk", in_one, self_qkv, preferred_element_type=jnp.float32
    ).astype(jnp.bfloat16)
    qkv_view = qkv_rows.reshape(captions, length, 3, local_heads, HEAD_SIZE)
    queries_one, keys_one, values_one = (qkv_view[:, :, 0], qkv_view[:, :, 1], qkv_view[:, :, 2])
    positions = jnp.arange(length)
    causal = jnp.broadcast_to(positions[:, None] >= positions[None, :], (captions, length, length))
    mixture_one, chances_one = attend_forward(queries_one, keys_one, values_one, causal, scaling)
    mixture_one = mixture_one.reshape(row_count, local_width)
    after_first_residual = (
        residual
        + branch_total(jnp.dot(mixture_one, self_output_weight, preferred_element_type=jnp.float32))
        + self_output_bias
    )
    second_normalized, inv_two = norm_parts(after_first_residual)
    in_two = (second_normalized * ln2_gain + ln2_bias).astype(jnp.bfloat16)
    second_query_rows = (
        jnp.dot(in_two, cross_query_weight, preferred_element_type=jnp.float32)
        .astype(jnp.bfloat16)
        .reshape(captions, length, local_heads, HEAD_SIZE)
    )
    image_full = lax.all_gather(image_tokens, "tensor", axis=2, tiled=True)
    image_count = image_full.shape[1]
    kv_rows = jnp.einsum(
        "cid,dtk->citk", image_full, cross_kv, preferred_element_type=jnp.float32
    ).astype(jnp.bfloat16)
    kv_view = kv_rows.reshape(captions, image_count, 2, local_heads, HEAD_SIZE)
    keys_two, values_two = (kv_view[:, :, 0], kv_view[:, :, 1])
    valid_keys = jnp.arange(image_count)[None, :] < image_counts[:, None]
    cross_mask = jnp.broadcast_to(valid_keys[:, None, :], (captions, length, image_count))
    mixture_two, chances_two = attend_forward(
        second_query_rows, keys_two, values_two, cross_mask, scaling
    )
    mixture_two = mixture_two.reshape(row_count, local_width)
    after_second_residual = (
        after_first_residual
        + branch_total(
            jnp.dot(mixture_two, cross_output_weight, preferred_element_type=jnp.float32)
        )
        + cross_output_bias
    )
    normed_three, inv_three = norm_parts(after_second_residual)
    in_three = (normed_three * ln3_gain + ln3_bias).astype(jnp.bfloat16)
    pre_act = jnp.dot(in_three, mlp_in, preferred_element_type=jnp.float32) + mlp_in_bias
    activated, gelu_pull = jax.vjp(partial(jax.nn.gelu, approximate=False), pre_act)
    act_low = activated.astype(jnp.bfloat16)
    result = (
        after_second_residual
        + branch_total(jnp.dot(act_low, mlp_out, preferred_element_type=jnp.float32))
        + mlp_out_bias
    )
    output = result.astype(jnp.bfloat16).reshape(tokens.shape)
    grad_rows = grad_out.astype(jnp.float32).reshape(row_count, model_width)
    grad_low = grad_rows.astype(jnp.bfloat16)
    grad_mlp_out_local = jnp.einsum(
        "rf,rd->fd", act_low, grad_low, preferred_element_type=jnp.float32
    )
    grad_hidden = jnp.einsum("rd,fd->rf", grad_low, mlp_out, preferred_element_type=jnp.float32)
    (grad_pre,) = gelu_pull(grad_hidden)
    grad_pre_low = grad_pre.astype(jnp.bfloat16)
    grad_mlp_in_bias = jnp.sum(grad_pre_low, axis=0, dtype=jnp.float32)
    grad_mlp_in_local = jnp.einsum(
        "rd,rf->df", in_three, grad_pre_low, preferred_element_type=jnp.float32
    )
    grad_in_three = input_total(
        jnp.einsum("rf,df->rd", grad_pre_low, mlp_in, preferred_element_type=jnp.float32)
    )
    grad_gain_three = jnp.sum(grad_in_three * normed_three, axis=0)
    grad_bias_three = jnp.sum(grad_in_three, axis=0)
    grad_two = grad_rows + norm_back(grad_in_three, normed_three, inv_three, ln3_gain)
    grad_two_low = grad_two.astype(jnp.bfloat16)
    grad_cross_bias = jnp.sum(grad_two, axis=0)
    grad_cross_out_local = jnp.einsum(
        "rk,rd->kd", mixture_two, grad_two_low, preferred_element_type=jnp.float32
    )
    grad_mix_two = jnp.einsum(
        "rd,kd->rk", grad_two_low, cross_output_weight, preferred_element_type=jnp.float32
    ).astype(jnp.bfloat16)
    grad_mix_two = grad_mix_two.reshape(captions, length, local_heads, HEAD_SIZE)
    grad_query_two, grad_keys_two, grad_values_two = attend_back(
        grad_mix_two, second_query_rows, keys_two, values_two, chances_two, scaling
    )
    grad_kv = jnp.stack([grad_keys_two, grad_values_two], axis=2).reshape(
        captions, image_count, 2, local_width
    )
    grad_cross_kv_local = jnp.einsum(
        "cid,citk->dtk", image_full, grad_kv, preferred_element_type=jnp.float32
    )
    image_terms = jnp.einsum("citk,dtk->cid", grad_kv, cross_kv, preferred_element_type=jnp.float32)
    grad_image = lax.psum_scatter(
        image_terms.astype(jnp.bfloat16), "tensor", scatter_dimension=2, tiled=True
    )
    query_rows_two = grad_query_two.reshape(row_count, local_width)
    grad_cross_q_local = jnp.einsum(
        "rd,rk->dk", in_two, query_rows_two, preferred_element_type=jnp.float32
    )
    grad_in_two = input_total(
        jnp.einsum(
            "rk,dk->rd", query_rows_two, cross_query_weight, preferred_element_type=jnp.float32
        )
    )
    grad_gain_two = jnp.sum(grad_in_two * second_normalized, axis=0)
    grad_bias_two = jnp.sum(grad_in_two, axis=0)
    grad_one = grad_two + norm_back(grad_in_two, second_normalized, inv_two, ln2_gain)
    grad_one_low = grad_one.astype(jnp.bfloat16)
    grad_self_bias = jnp.sum(grad_one, axis=0)
    grad_self_out_local = jnp.einsum(
        "rk,rd->kd", mixture_one, grad_one_low, preferred_element_type=jnp.float32
    )
    grad_mix_one = jnp.einsum(
        "rd,kd->rk", grad_one_low, self_output_weight, preferred_element_type=jnp.float32
    ).astype(jnp.bfloat16)
    grad_mix_one = grad_mix_one.reshape(captions, length, local_heads, HEAD_SIZE)
    grad_query_one, grad_keys_one, grad_values_one = attend_back(
        grad_mix_one, queries_one, keys_one, values_one, chances_one, scaling
    )
    grad_qkv = jnp.stack([grad_query_one, grad_keys_one, grad_values_one], axis=2).reshape(
        row_count, 3, local_width
    )
    grad_self_qkv_local = jnp.einsum(
        "rd,rtk->dtk", in_one, grad_qkv, preferred_element_type=jnp.float32
    )
    grad_in_one = input_total(
        jnp.einsum("rtk,dtk->rd", grad_qkv, self_qkv, preferred_element_type=jnp.float32)
    )
    grad_gain_one = jnp.sum(grad_in_one * normed_one, axis=0)
    grad_bias_one = jnp.sum(grad_in_one, axis=0)
    grad_tokens = (
        (grad_one + norm_back(grad_in_one, normed_one, inv_one, ln1_gain))
        .astype(jnp.bfloat16)
        .reshape(tokens.shape)
    )
    grad_out_bias = jnp.sum(grad_rows, axis=0)
    (
        grad_self_qkv,
        grad_self_out,
        grad_cross_q,
        grad_cross_kv,
        grad_cross_out,
        grad_mlp_in,
        grad_mlp_out,
    ) = (
        lax.psum_scatter(grad_self_qkv_local, "dp", scatter_dimension=0, tiled=True),
        lax.psum_scatter(grad_self_out_local, "dp", scatter_dimension=1, tiled=True),
        lax.psum_scatter(grad_cross_q_local, "dp", scatter_dimension=0, tiled=True),
        lax.psum_scatter(grad_cross_kv_local, "dp", scatter_dimension=0, tiled=True),
        lax.psum_scatter(grad_cross_out_local, "dp", scatter_dimension=1, tiled=True),
        lax.psum_scatter(grad_mlp_in_local, "dp", scatter_dimension=0, tiled=True),
        lax.psum_scatter(grad_mlp_out_local, "dp", scatter_dimension=1, tiled=True),
    )
    (
        grad_gain_one,
        grad_bias_one,
        grad_self_bias,
        grad_gain_two,
        grad_bias_two,
        grad_cross_bias,
        grad_gain_three,
        grad_bias_three,
        grad_mlp_in_bias,
        grad_out_bias,
    ) = lax.psum(
        (
            grad_gain_one,
            grad_bias_one,
            grad_self_bias,
            grad_gain_two,
            grad_bias_two,
            grad_cross_bias,
            grad_gain_three,
            grad_bias_three,
            grad_mlp_in_bias,
            grad_out_bias,
        ),
        "dp",
    )
    return (
        output,
        grad_tokens,
        grad_image,
        grad_gain_one,
        grad_bias_one,
        grad_self_qkv,
        grad_self_out,
        grad_self_bias,
        grad_gain_two,
        grad_bias_two,
        grad_cross_q,
        grad_cross_kv,
        grad_cross_out,
        grad_cross_bias,
        grad_gain_three,
        grad_bias_three,
        grad_mlp_in,
        grad_mlp_in_bias,
        grad_mlp_out,
        grad_out_bias,
    )


def solution(mesh):
    return jax.shard_map(
        local,
        mesh=mesh,
        in_specs=(
            P("dp", None, None),
            P("dp", None, "tensor"),
            P("dp"),
            P(),
            P(),
            P(None, None, "tensor"),
            P("tensor", None),
            P(),
            P(),
            P(),
            P(None, "tensor"),
            P(None, None, "tensor"),
            P("tensor", None),
            P(),
            P(),
            P(),
            P(None, "tensor"),
            P("tensor"),
            P("tensor", None),
            P(),
            P("dp", None, None),
        ),
        out_specs=(
            P("dp", None, None),
            P("dp", None, None),
            P("dp", None, "tensor"),
            P(),
            P(),
            P("dp", None, "tensor"),
            P("tensor", "dp"),
            P(),
            P(),
            P(),
            P("dp", "tensor"),
            P("dp", None, "tensor"),
            P("tensor", "dp"),
            P(),
            P(),
            P(),
            P("dp", "tensor"),
            P("tensor"),
            P("tensor", "dp"),
            P(),
        ),
        check_vma=False,
    )
```

profile of v0, /device:TPU:0, one launch (start us, length us, event | category | flops | bytes accessed | tf_op | source)
XLA Modules:
  0.0 956.3 jit_solution(9521117675636398474)
XLA Ops:
  14.8 4.2 reshape.186
  31.6 3.6 fusion.59
  44.7 44.1 %all-reduce.8.cloned.1.call-done = bf16[1024,768]{1,0:T(8,128)(2,1)} async-done(((bf16[1024,768]{1,0:T(8,128)(2,1)}), bf16[1024,768]{1,0:T(8,128)(2,1)}) %all-reduce.8.cloned.1.call-update) | async-done | bytes 1572880 | tf_op jit(solution)/shard_map/psum | solution.py:26
  97.8 39.0 %all-gather.2.cloned.1.call-done = bf16[16,256,768]{1,2,0:T(8,128)(2,1)} async-done(((bf16[16,256,192]{1,2,0:T(8,128)(2,1)}), bf16[16,256,768]{1,2,0:T(8,128)(2,1)}) %all-gather.2.cloned.1.call-update) | async-done | bytes 6291472 | tf_op jit(solution)/shard_map/all_gather | solution.py:130
  136.8 5.6 fusion.46
  157.7 40.0 %all-reduce.10.cloned.1.call-done = bf16[1024,768]{1,0:T(8,128)(2,1)} async-done(((bf16[1024,768]{1,0:T(8,128)(2,1)}), bf16[1024,768]{1,0:T(8,128)(2,1)}) %all-reduce.10.cloned.1.call-update) | async-done | bytes 1572880 | tf_op jit(solution)/shard_map/psum | solution.py:26
  204.9 10.3 %convert_reduce_fusion.5 = (f32[768]{0:T(1024)}, bf16[1024,768]{1,0:T(8,128)(2,1)S(1)}, f32[1024,768]{1,0:T(8,128)}) fusion(f32[1024,768]{1,0:T(8,128)S(1)} %fusion.100, f32[768]{0:T(1024)S(1)} %copy-done.59, bf16[1024,768]{1,0:T(8,128)(2,1)S(1)} %copy-done.29, bf16[768,768]{1,0:T(8,128)(2,1)S(1)} %copy-done), kind=kOutput, calls=%fused_computation.59 | convolution fusion | flops 1266941184 | bytes 10622976 | tf_op jit(solution)/shard_map/rd,fd->rf/dot_general | solution.py:166
  219.3 4.4 multiply_convert_fusion.2
  223.7 38.3 %all-reduce.12.cloned.1.call-done = bf16[1024,768]{1,0:T(8,128)(2,1)} async-done(((bf16[1024,768]{1,0:T(8,128)(2,1)}), bf16[1024,768]{1,0:T(8,128)(2,1)}) %all-reduce.12.cloned.1.call-update) | async-done | bytes 1572880 | tf_op jit(solution)/shard_map/psum | solution.py:30
  262.0 4.4 fusion.29
  275.1 4.0 multiply_reduce_fusion
  290.8 4.1 convolution_convert_fusion.3
  299.2 11.6 %reduce-scatter.25.cloned.1.call-start = ((), (), s32[]{:S(2)}) async-start(), calls=%async_computation.18 | async-start | bytes 884736
  310.8 23.0 %all-reduce.14.cloned.1.call-done = bf16[1024,768]{1,0:T(8,128)(2,1)} async-done(((bf16[1024,768]{1,0:T(8,128)(2,1)}), bf16[1024,768]{1,0:T(8,128)(2,1)}) %all-reduce.14.cloned.1.call-update) | async-done | bytes 1572880 | tf_op jit(solution)/shard_map/psum | solution.py:30
  333.8 4.2 fusion.30
  347.7 7.1 fusion.2
  363.3 3.7 fusion.60
  391.8 3.8 bitcast_convert_fusion.1
  399.5 4.8 fusion.103
  404.6 4.7 fusion.102
  409.4 4.7 fusion.50
  414.1 7.4 bitcast_convert_fusion
  425.1 40.9 %reduce-scatter.25.cloned.1.call-done = f32[96,192]{1,0:T(8,128)} async-done(((f32[768,192]{1,0:T(8,128)}), f32[96,192]{1,0:T(8,128)}) %reduce-scatter.25.cloned.1.call-update) | async-done | bytes 73744
  467.6 65.5 %reduce-scatter.27.cloned.1.call-done = f32[96,384]{1,0:T(8,128)} async-done(((f32[768,384]{1,0:T(8,128)}), f32[96,384]{1,0:T(8,128)}) %reduce-scatter.27.cloned.1.call-update) | async-done | bytes 147472
  535.0 68.7 %all-reduce.16.cloned.1.call-done = (bf16[1024,768]{1,0:T(8,128)(2,1)}, bf16[1024,768]{1,0:T(8,128)(2,1)}) async-done(((bf16[1024,768]{1,0:T(8,128)(2,1)}, bf16[1024,768]{1,0:T(8,128)(2,1)}), (bf16[1024,768]{1,0:T(8,128)(2,1)}, bf16[1024,768]{1,0:T(8,128)(2,1)})) %all-reduce.16.cloned.1.call-update) | async-done | bytes 3145744 | tf_op jit(solution)/shard_map/psum | solution.py:26
  606.6 38.2 %all-reduce = (f32[768]{0:T(1024)}, f32[768]{0:T(1024)}, f32[768]{0:T(1024)}, f32[768]{0:T(1024)}, f32[768]{0:T(1024)}, /*index=5*/f32[768]{0:T(1024)}, f32[768]...) all-reduce(f32[768]{0:T(1024)S(1)} %get-tuple-element.84, ...), channel_id=1, replica_groups=mesh['dp'=8,'tensor'=4] {'dp'}, use_global_device_ids=true, to_apply=%region_26.27 | all-reduce | flops 7680 | bytes 61440 | tf_op jit(solution)/shard_map/psum | solution.py:270
  644.8 4.1 add_convert_fusion.1
  651.1 19.6 %reduce-scatter.19.cloned.1.call-done = f32[96,192]{1,0:T(8,128)} async-done(((f32[768,192]{1,0:T(8,128)}), f32[96,192]{1,0:T(8,128)}) %reduce-scatter.19.cloned.1.call-update) | async-done | bytes 73744 | tf_op jit(solution)/shard_map/reduce_scatter | solution.py:253
  670.7 73.0 %reduce-scatter.23.cloned.1.call-done = f32[768,96]{0,1:T(8,128)} async-done(((f32[768,768]{0,1:T(8,128)}), f32[768,96]{0,1:T(8,128)}) %reduce-scatter.23.cloned.1.call-update) | async-done | bytes 294928 | tf_op jit(solution)/shard_map/reduce_scatter | solution.py:257
  743.7 72.7 %reduce-scatter.21.cloned.1.call-done = f32[96,768]{1,0:T(8,128)} async-done(((f32[768,768]{1,0:T(8,128)}), f32[96,768]{1,0:T(8,128)}) %reduce-scatter.21.cloned.1.call-update) | async-done | bytes 294928 | tf_op jit(solution)/shard_map/reduce_scatter | solution.py:256
  816.4 73.0 %reduce-scatter.17.cloned.1.call-done = f32[96,3,192]{2,0,1:T(8,128)} async-done(((f32[768,3,192]{2,0,1:T(8,128)}), f32[96,3,192]{2,0,1:T(8,128)}) %reduce-scatter.17.cloned.1.call-update) | async-done | bytes 221200 | tf_op jit(solution)/shard_map/reduce_scatter | solution.py:251
  889.3 60.2 %reduce-scatter.15.cloned.1.call-done = bf16[16,256,192]{1,2,0:T(8,128)(2,1)} async-done(((bf16[16,256,768]{1,2,0:T(8,128)(2,1)}), bf16[16,256,192]{1,2,0:T(8,128)(2,1)}) %reduce-scatter.15.cloned.1.call-update) | async-done | bytes 1572880 | tf_op jit(solution)/shard_map/reduce_scatter | solution.py:198
  (256 shorter events, 148.6 us)
Async XLA Ops:
  7.2 197.1 %copy-start = (bf16[768,768]{1,0:T(8,128)(2,1)S(1)}, bf16[768,768]{1,0:T(8,128)(2,1)}, u32[]{:S(2)}) copy-start(bf16[768,768]{1,0:T(8,128)(2,1)} %param.39) | copy-start | bytes 3538948
  7.2 81.6 %all-reduce.8.cloned.1.call-start = ((), (), s32[]{:S(2)}) async-start(), calls=%async_computation.8 | async-start | bytes 3145728 | tf_op jit(solution)/shard_map/psum | solution.py:26
  37.8 6.3 copy-start.67
  37.8 51.0 %copy-start.36 = (f32[768]{0:T(1024)S(1)}, f32[768]{0:T(1024)}, u32[]{:S(2)}) copy-start(f32[768]{0:T(1024)} %param.28) | copy-start | bytes 9220
  43.1 93.8 %all-gather.2.cloned.1.call-start = ((), (), s32[]{:S(2)}) async-start(), calls=%async_computation.9 | async-start | bytes 7864320 | tf_op jit(solution)/shard_map/all_gather | solution.py:130
  43.8 153.9 %all-reduce.10.cloned.1.call-start = ((), (), s32[]{:S(2)}) async-start(), calls=%async_computation.10 | async-start | bytes 3145728 | tf_op jit(solution)/shard_map/psum | solution.py:26
  136.8 5.6 copy-start.14
  151.8 45.9 %copy-start.61 = (f32[768]{0:T(1024)S(1)}, f32[768]{0:T(1024)}, u32[]{:S(2)}) copy-start(f32[768]{0:T(1024)} %param.34) | copy-start | bytes 9220
  154.7 107.3 %all-reduce.12.cloned.1.call-start = ((), (), s32[]{:S(2)}) async-start(), calls=%async_computation.11 | async-start | bytes 3145728 | tf_op jit(solution)/shard_map/psum | solution.py:30
  204.9 10.3 %copy-start.25 = (f32[1024,768]{1,0:T(8,128)}, f32[1024,768]{1,0:T(8,128)S(1)}, u32[]{:S(2)}) copy-start(f32[1024,768]{1,0:T(8,128)S(1)} %fusion.100) | copy-start | bytes 9437188
  218.9 114.9 %all-reduce.14.cloned.1.call-start = ((), (), s32[]{:S(2)}) async-start(), calls=%async_computation.12 | async-start | bytes 3145728 | tf_op jit(solution)/shard_map/psum | solution.py:30
  290.7 132.7 %reduce-scatter.29.cloned.1.call-start = ((), (), s32[]{:S(2)}) async-start(), calls=%async_computation.20 | async-start | bytes 884736
  297.5 36.3 %copy-start.42 = (f32[1024]{0:T(1024)S(1)}, f32[1024]{0:T(1024)}, u32[]{:S(2)}) copy-start(f32[1024]{0:T(1024)} %copy-done.41) | copy-start | bytes 12292
  299.2 166.8 %reduce-scatter.25.cloned.1.call-start = ((), (), s32[]{:S(2)}) async-start(), calls=%async_computation.18 | async-start | bytes 884736
  344.8 188.3 %reduce-scatter.27.cloned.1.call-start = ((), (), s32[]{:S(2)}) async-start(), calls=%async_computation.19 | async-start | bytes 1327104
  347.7 7.1 copy-start.71
  357.5 246.1 %all-reduce.16.cloned.1.call-start = ((), (), s32[]{:S(2)}) async-start(), calls=%async_computation.21 | async-start | bytes 6291456 | tf_op jit(solution)/shard_map/psum | solution.py:26
  395.5 275.1 %reduce-scatter.19.cloned.1.call-start = ((), (), s32[]{:S(2)}) async-start(), calls=%async_computation.15 | async-start | bytes 884736 | tf_op jit(solution)/shard_map/reduce_scatter | solution.py:253
  399.4 344.2 %reduce-scatter.23.cloned.1.call-start = ((), (), s32[]{:S(2)}) async-start(), calls=%async_computation.17 | async-start | bytes 2654208 | tf_op jit(solution)/shard_map/reduce_scatter | solution.py:257
  404.3 412.1 %reduce-scatter.21.cloned.1.call-start = ((), (), s32[]{:S(2)}) async-start(), calls=%async_computation.16 | async-start | bytes 2654208 | tf_op jit(solution)/shard_map/reduce_scatter | solution.py:256
  409.3 480.0 %reduce-scatter.17.cloned.1.call-start = ((), (), s32[]{:S(2)}) async-start(), calls=%async_computation.14 | async-start | bytes 2654208 | tf_op jit(solution)/shard_map/reduce_scatter | solution.py:251
  414.1 535.5 %reduce-scatter.15.cloned.1.call-start = ((), (), s32[]{:S(2)}) async-start(), calls=%async_computation.13 | async-start | bytes 7864320 | tf_op jit(solution)/shard_map/reduce_scatter | solution.py:198
  421.5 182.1 %copy-start.40 = (f32[1024]{0:T(1024)S(1)}, f32[1024]{0:T(1024)}, u32[]{:S(2)}) copy-start(f32[1024]{0:T(1024)} %copy-done.39) | copy-start | bytes 12292
  421.5 182.1 %copy-start.46 = (f32[768]{0:T(1024)S(1)}, f32[768]{0:T(1024)}, u32[]{:S(2)}) copy-start(f32[768]{0:T(1024)} %param.24) | copy-start | bytes 9220
  421.6 185.0 %copy-start.53 = (f32[768]{0:T(1024)S(1)}, f32[768]{0:T(1024)}, u32[]{:S(2)}) copy-start(f32[768]{0:T(1024)} %get-tuple-element.107) | copy-start | bytes 9220
  421.6 185.0 %copy-start.54 = (f32[768]{0:T(1024)S(1)}, f32[768]{0:T(1024)}, u32[]{:S(2)}) copy-start(f32[768]{0:T(1024)} %get-tuple-element.80) | copy-start | bytes 9220
  421.6 185.0 %copy-start.55 = (f32[768]{0:T(1024)S(1)}, f32[768]{0:T(1024)}, u32[]{:S(2)}) copy-start(f32[768]{0:T(1024)} %get-tuple-element.90) | copy-start | bytes 9220
  421.6 185.0 %copy-start.56 = (f32[768]{0:T(1024)S(1)}, f32[768]{0:T(1024)}, u32[]{:S(2)}) copy-start(f32[768]{0:T(1024)} %get-tuple-element.109) | copy-start | bytes 9220
  421.6 185.0 %copy-start.57 = (f32[768]{0:T(1024)S(1)}, f32[768]{0:T(1024)}, u32[]{:S(2)}) copy-start(f32[768]{0:T(1024)} %get-tuple-element.82) | copy-start | bytes 9220
  421.6 185.0 %copy-start.58 = (f32[768]{0:T(1024)S(1)}, f32[768]{0:T(1024)}, u32[]{:S(2)}) copy-start(f32[768]{0:T(1024)} %get-tuple-element.89) | copy-start | bytes 9220
  421.6 185.0 %copy-start.63 = (f32[768]{0:T(1024)S(1)}, f32[768]{0:T(1024)}, u32[]{:S(2)}) copy-start(f32[768]{0:T(1024)} %get-tuple-element.104) | copy-start | bytes 9220
  421.6 223.2 %copy-start.66 = (f32[768]{0:T(1024)S(1)}, f32[768]{0:T(1024)}, u32[]{:S(2)}) copy-start(f32[768]{0:T(1024)} %param.40) | copy-start | bytes 9220
  (55 other events, 148.4 us)
Sparse Core Ops, SparseCore 0:
  43.2 45.5 all-reduce.7
  90.4 46.4 all-gather.1
  154.8 42.8 all-reduce.9
  219.1 42.8 all-reduce.11
  290.9 42.9 all-reduce.13
  337.0 63.3 reduce-scatter.28
  403.6 62.2 reduce-scatter.24
  469.4 63.7 reduce-scatter.26
  536.1 67.4 all-reduce.15
  607.4 63.2 reduce-scatter.18
  674.7 68.8 reduce-scatter.22
  747.6 68.7 reduce-scatter.20
  820.4 68.8 reduce-scatter.16
  892.3 57.2 reduce-scatter.14
where the time goes:
time: 964 us; the launch traced here: 956 us
  waiting for transfers between devices  659 us (68%)
  matrix products  105 us (11%)
  local copies, waits for them, and re-layouts  71.6 us (7%)
  other arithmetic  54.1 us (6%)
  blocking collectives  38.2 us (4%)
  between operations  15 us (2%)
  starting transfers between devices  13.1 us (1%)
    psum x3, waiting for transfers between devices, branch_total(): lax.psum(term_rows.astype(jnp.bfloat16), 'tensor').astype(jnp.float32)  153 us
    unnamed x17, waiting for transfers between devices  107 us
    reduce_scatter x1, waiting for transfers between devices, local(): lax.psum_scatter(grad_mlp_out_local, 'dp', scatter_dimension=1, tiled=True)  73 us
    reduce_scatter x1, waiting for transfers between devices, local(): lax.psum_scatter(grad_self_qkv_local, 'dp', scatter_dimension=0, tiled=True)  73 us
    reduce_scatter x1, waiting for transfers between devices, local(): lax.psum_scatter(grad_mlp_in_local, 'dp', scatter_dimension=0, tiled=True)  72.7 us
    psum x2, waiting for transfers between devices, input_total(): lax.psum(term_rows.astype(jnp.bfloat16), 'tensor').astype(jnp.float32)  61.2 us
    reduce_scatter x1, waiting for transfers between devices, local(): lax.psum_scatter(image_terms.astype(jnp.bfloat16), 'tensor', scatter_dime...  60.2 us
    all_gather x1, waiting for transfers between devices, local(): image_full = lax.all_gather(image_tokens, 'tensor', axis=2, tiled=True)  39 us
  transfers between devices with their start and end apart: 14, of which 13 were waited for; matrix products, arithmetic and copies ran while one was open for 13% of the time, Pallas kernels for 0%

commit v1 on v0

--- a/solution.py
+++ b/solution.py
@@ -5,6 +5,11 @@
 from jax.sharding import PartitionSpec as P
 
 HEAD_SIZE = 64
+
+
+def gather_and_add(block, axis):
+    shards = lax.all_gather(block, axis)
+    return jnp.sum(shards, axis=0)
 
 
 def norm_parts(values):
@@ -23,7 +28,7 @@
 
 
 def branch_total(term_rows):
-    return lax.psum(term_rows.astype(jnp.bfloat16), "tensor").astype(jnp.float32)
+    return gather_and_add(term_rows.astype(jnp.bfloat16), "tensor").astype(jnp.float32)
 
 
 def input_total(term_rows):

time: 964 us -> 1010 us (1.048)
  other arithmetic: 54.1 us -> 80.8 us
  waiting for transfers between devices: 659 us -> 682 us
  starting transfers between devices: 13.1 us -> 2.19 us
    psum x3 -> x0, waiting for transfers between devices: 153 us -> none  [branch_total(): lax.psum(term_rows.astype(jnp.bfloat16), 'tensor').astype(jnp.float32)]
    all_gather x0 -> x3, waiting for transfers between devices: none -> 137 us  [gather_and_add(): shards = lax.all_gather(block, axis)]
    reduce_scatter x1, waiting for transfers between devices: 19.6 us -> 58.9 us  [local(): lax.psum_scatter(grad_cross_q_local, 'dp', scatter_dimension=0, tiled=True)]
    psum x2 -> x3, waiting for transfers between devices: 61.2 us -> 93 us  [input_total(): lax.psum(term_rows.astype(jnp.bfloat16), 'tensor').astype(jnp.float32)]
    unnamed x17 -> x18, waiting for transfers between devices: 107 us -> 88.4 us
    reduce_sum x0 -> x3, other arithmetic: none -> 15.4 us  [gather_and_add(): return jnp.sum(shards, axis=0)]
    all_gather x1, waiting for transfers between devices: 39 us -> 27 us  [local(): image_full = lax.all_gather(image_tokens, 'tensor', axis=2, tiled=True)]
    unnamed x3, starting transfers between devices: 11.7 us -> 0.34 us
  transfers between devices with their start and end apart: 14 -> 15, of which waited for: 13 -> 14; matrix products, arithmetic and copies ran while one was open for 13% -> 14% of each run, Pallas kernels for 0% -> 0%
where the time goes in v1:
time: 1010 us; the launch traced here: 998 us
  waiting for transfers between devices  682 us (68%)
  matrix products  106 us (10%)
  other arithmetic  80.8 us (8%)
  local copies, waits for them, and re-layouts  72.5 us (7%)
  blocking collectives  38.1 us (4%)
  between operations  15.3 us (2%)
    all_gather x3, waiting for transfers between devices, gather_and_add(): shards = lax.all_gather(block, axis)  137 us
    psum x3, waiting for transfers between devices, input_total(): lax.psum(term_rows.astype(jnp.bfloat16), 'tensor').astype(jnp.float32)  93 us
    unnamed x18, waiting for transfers between devices  88.4 us
    reduce_scatter x1, waiting for transfers between devices, local(): lax.psum_scatter(grad_self_qkv_local, 'dp', scatter_dimension=0, tiled=True)  72.9 us
    reduce_scatter x1, waiting for transfers between devices, local(): lax.psum_scatter(grad_mlp_in_local, 'dp', scatter_dimension=0, tiled=True)  72.9 us
    reduce_scatter x1, waiting for transfers between devices, local(): lax.psum_scatter(grad_mlp_out_local, 'dp', scatter_dimension=1, tiled=True)  72.6 us
    reduce_scatter x1, waiting for transfers between devices, local(): lax.psum_scatter(image_terms.astype(jnp.bfloat16), 'tensor', scatter_dime...  60.2 us
    reduce_scatter x1, waiting for transfers between devices, local(): lax.psum_scatter(grad_cross_q_local, 'dp', scatter_dimension=0, tiled=True)  58.9 us
  transfers between devices with their start and end apart: 15, of which 14 were waited for; matrix products, arithmetic and copies ran while one was open for 14% of the time, Pallas kernels for 0%

profile of v1, /device:TPU:0, one launch (start us, length us, event | category | flops | bytes accessed | tf_op | source)
XLA Modules:
  0.0 997.7 jit_solution(14129401830106081236)
XLA Ops:
  14.8 4.2 reshape.302
  44.8 47.6 %all-gather.10.cloned.1.call-done = bf16[4096,768]{1,0:T(8,128)(2,1)} async-done(((bf16[1024,768]{1,0:T(8,128)(2,1)}), bf16[4096,768]{1,0:T(8,128)(2,1)}) %all-gather.10.cloned.1.call-update) | async-done | bytes 6291472 | tf_op jit(solution)/shard_map/all_gather | solution.py:11
  92.4 5.3 reduce_sum.273
  113.3 27.0 %all-gather.8.cloned.1.call-done = bf16[16,256,768]{1,2,0:T(8,128)(2,1)} async-done(((bf16[16,256,192]{1,2,0:T(8,128)(2,1)}), bf16[16,256,768]{1,2,0:T(8,128)(2,1)}) %all-gather.8.cloned.1.call-update) | async-done | bytes 6291472 | tf_op jit(solution)/shard_map/all_gather | solution.py:135
  140.3 5.6 fusion.49
  161.2 43.5 %all-gather.12.cloned.1.call-done = bf16[4096,768]{1,0:T(8,128)(2,1)} async-done(((bf16[1024,768]{1,0:T(8,128)(2,1)}), bf16[4096,768]{1,0:T(8,128)(2,1)}) %all-gather.12.cloned.1.call-update) | async-done | bytes 6291472 | tf_op jit(solution)/shard_map/all_gather | solution.py:11
  204.8 5.4 reduce_sum.277
  210.1 4.1 add_convert_fusion
  224.4 10.2 %convert_reduce_fusion.5 = (f32[768]{0:T(1024)}, bf16[1024,768]{1,0:T(8,128)(2,1)S(1)}, f32[1024,768]{1,0:T(8,128)}) fusion(f32[1024,768]{1,0:T(8,128)S(1)} %fusion.93, f32[768]{0:T(1024)S(1)} %copy-done.57, bf16[1024,768]{1,0:T(8,128)(2,1)S(1)} %copy-done.25, bf16[768,768]{1,0:T(8,128)(2,1)S(1)} %copy-done), kind=kOutput, calls=%fused_computation.64 | convolution fusion | flops 1266941184 | bytes 10622976 | tf_op jit(solution)/shard_map/rd,fd->rf/dot_general | solution.py:171
  239.0 42.5 %all-reduce.5.cloned.1.call-done = bf16[1024,768]{1,0:T(8,128)(2,1)} async-done(((bf16[1024,768]{1,0:T(8,128)(2,1)}), bf16[1024,768]{1,0:T(8,128)(2,1)}) %all-reduce.5.cloned.1.call-update) | async-done | bytes 1572880 | tf_op jit(solution)/shard_map/psum | solution.py:35
  281.5 4.1 fusion.29
  293.6 4.0 multiply_reduce_fusion
  313.2 39.1 %all-reduce.7.cloned.1.call-done = bf16[1024,768]{1,0:T(8,128)(2,1)} async-done(((bf16[1024,768]{1,0:T(8,128)(2,1)}), bf16[1024,768]{1,0:T(8,128)(2,1)}) %all-reduce.7.cloned.1.call-update) | async-done | bytes 1572880 | tf_op jit(solution)/shard_map/psum | solution.py:35
  352.3 4.4 fusion.30
  394.1 3.8 bitcast_convert_fusion.1
  406.0 7.0 fusion.2
  425.9 4.8 fusion.111
  430.8 5.3 fusion.92
  436.2 4.7 fusion.54
  441.2 7.4 bitcast_convert_fusion
  452.2 11.5 %all-reduce.9.cloned.1.call-done = bf16[1024,768]{1,0:T(8,128)(2,1)} async-done(((bf16[1024,768]{1,0:T(8,128)(2,1)}), bf16[1024,768]{1,0:T(8,128)(2,1)}) %all-reduce.9.cloned.1.call-update) | async-done | bytes 1572880 | tf_op jit(solution)/shard_map/psum | solution.py:35
  466.7 38.1 %all-reduce = (f32[768]{0:T(1024)}, f32[768]{0:T(1024)}, f32[768]{0:T(1024)}, f32[768]{0:T(1024)}, f32[768]{0:T(1024)}, /*index=5*/f32[768]{0:T(1024)}, f32[768]...) all-reduce(f32[768]{0:T(1024)S(1)} %get-tuple-element.84, ...), channel_id=1, replica_groups=mesh['dp'=8,'tensor'=4] {'dp'}, use_global_device_ids=true, to_apply=%region_26.27 | all-reduce | flops 7680 | bytes 61440 | tf_op jit(solution)/shard_map/psum | solution.py:275
  504.8 3.8 fusion.18
  508.6 21.8 %reduce-scatter.25.cloned.1.call-done = f32[96,192]{1,0:T(8,128)} async-done(((f32[768,192]{1,0:T(8,128)}), f32[96,192]{1,0:T(8,128)}) %reduce-scatter.25.cloned.1.call-update) | async-done | bytes 73744
  532.0 65.7 %reduce-scatter.27.cloned.1.call-done = f32[96,384]{1,0:T(8,128)} async-done(((f32[768,384]{1,0:T(8,128)}), f32[96,384]{1,0:T(8,128)}) %reduce-scatter.27.cloned.1.call-update) | async-done | bytes 147472
  599.6 45.5 %all-gather.14.cloned.1.call-done = bf16[4096,768]{1,0:T(8,128)(2,1)} async-done(((bf16[1024,768]{1,0:T(8,128)(2,1)}), bf16[4096,768]{1,0:T(8,128)(2,1)}) %all-gather.14.cloned.1.call-update) | async-done | bytes 6291472 | tf_op jit(solution)/shard_map/all_gather | solution.py:11
  645.1 4.7 reduce_sum.280
  653.4 58.9 %reduce-scatter.19.cloned.1.call-done = f32[96,192]{1,0:T(8,128)} async-done(((f32[768,192]{1,0:T(8,128)}), f32[96,192]{1,0:T(8,128)}) %reduce-scatter.19.cloned.1.call-update) | async-done | bytes 73744 | tf_op jit(solution)/shard_map/reduce_scatter | solution.py:258
  712.2 72.6 %reduce-scatter.23.cloned.1.call-done = f32[768,96]{0,1:T(8,128)} async-done(((f32[768,768]{0,1:T(8,128)}), f32[768,96]{0,1:T(8,128)}) %reduce-scatter.23.cloned.1.call-update) | async-done | bytes 294928 | tf_op jit(solution)/shard_map/reduce_scatter | solution.py:262
  784.8 72.9 %reduce-scatter.21.cloned.1.call-done = f32[96,768]{1,0:T(8,128)} async-done(((f32[768,768]{1,0:T(8,128)}), f32[96,768]{1,0:T(8,128)}) %reduce-scatter.21.cloned.1.call-update) | async-done | bytes 294928 | tf_op jit(solution)/shard_map/reduce_scatter | solution.py:261
  857.7 72.9 %reduce-scatter.17.cloned.1.call-done = f32[96,3,192]{2,0,1:T(8,128)} async-done(((f32[768,3,192]{2,0,1:T(8,128)}), f32[96,3,192]{2,0,1:T(8,128)}) %reduce-scatter.17.cloned.1.call-update) | async-done | bytes 221200 | tf_op jit(solution)/shard_map/reduce_scatter | solution.py:256
  930.6 60.2 %reduce-scatter.15.cloned.1.call-done = bf16[16,256,192]{1,2,0:T(8,128)(2,1)} async-done(((bf16[16,256,768]{1,2,0:T(8,128)(2,1)}), bf16[16,256,192]{1,2,0:T(8,128)(2,1)}) %reduce-scatter.15.cloned.1.call-update) | async-done | bytes 1572880 | tf_op jit(solution)/shard_map/reduce_scatter | solution.py:203
  (265 shorter events, 173.9 us)
Async XLA Ops:
  7.2 216.4 %copy-start = (bf16[768,768]{1,0:T(8,128)(2,1)S(1)}, bf16[768,768]{1,0:T(8,128)(2,1)}, u32[]{:S(2)}) copy-start(bf16[768,768]{1,0:T(8,128)(2,1)} %param.39) | copy-start | bytes 3538948
  7.2 85.1 %all-gather.10.cloned.1.call-start = ((), (), s32[]{:S(2)}) async-start(), calls=%async_computation.17 | async-start | bytes 7864320 | tf_op jit(solution)/shard_map/all_gather | solution.py:11
  37.8 6.3 copy-start.64
  43.1 97.2 %all-gather.8.cloned.1.call-start = ((), (), s32[]{:S(2)}) async-start(), calls=%async_computation.8 | async-start | bytes 7864320 | tf_op jit(solution)/shard_map/all_gather | solution.py:135
  43.9 160.9 %all-gather.12.cloned.1.call-start = ((), (), s32[]{:S(2)}) async-start(), calls=%async_computation.18 | async-start | bytes 7864320 | tf_op jit(solution)/shard_map/all_gather | solution.py:11
  140.3 5.6 copy-start.12
  158.2 123.2 %all-reduce.5.cloned.1.call-start = ((), (), s32[]{:S(2)}) async-start(), calls=%async_computation.9 | async-start | bytes 3145728 | tf_op jit(solution)/shard_map/psum | solution.py:35
  224.4 10.2 %copy-start.20 = (f32[1024,768]{1,0:T(8,128)}, f32[1024,768]{1,0:T(8,128)S(1)}, u32[]{:S(2)}) copy-start(f32[1024,768]{1,0:T(8,128)S(1)} %fusion.93) | copy-start | bytes 9437188
  238.4 113.8 %all-reduce.7.cloned.1.call-start = ((), (), s32[]{:S(2)}) async-start(), calls=%async_computation.10 | async-start | bytes 3145728 | tf_op jit(solution)/shard_map/psum | solution.py:35
  309.2 43.1 %copy-start.43 = (f32[768]{0:T(1024)S(1)}, f32[768]{0:T(1024)}, u32[]{:S(2)}) copy-start(f32[768]{0:T(1024)} %param.29) | copy-start | bytes 9220
  309.2 43.1 %copy-start.45 = (f32[1024]{0:T(1024)S(1)}, f32[1024]{0:T(1024)}, u32[]{:S(2)}) copy-start(f32[1024]{0:T(1024)} %div.64) | copy-start | bytes 12292
  309.2 43.1 %copy-start.47 = (f32[1024]{0:T(1024)S(1)}, f32[1024]{0:T(1024)}, u32[]{:S(2)}) copy-start(f32[1024]{0:T(1024)} %rsqrt.37) | copy-start | bytes 12292
  309.2 141.4 %reduce-scatter.29.cloned.1.call-start = ((), (), s32[]{:S(2)}) async-start(), calls=%async_computation.22 | async-start | bytes 884736
  313.0 150.7 %all-reduce.9.cloned.1.call-start = ((), (), s32[]{:S(2)}) async-start(), calls=%async_computation.11 | async-start | bytes 3145728 | tf_op jit(solution)/shard_map/psum | solution.py:35
  398.0 132.4 %reduce-scatter.25.cloned.1.call-start = ((), (), s32[]{:S(2)}) async-start(), calls=%async_computation.20 | async-start | bytes 884736
  403.0 194.7 %reduce-scatter.27.cloned.1.call-start = ((), (), s32[]{:S(2)}) async-start(), calls=%async_computation.21 | async-start | bytes 1327104
  406.0 7.0 copy-start.70
  415.7 229.4 %all-gather.14.cloned.1.call-start = ((), (), s32[]{:S(2)}) async-start(), calls=%async_computation.19 | async-start | bytes 7864320 | tf_op jit(solution)/shard_map/all_gather | solution.py:11
  422.8 289.4 %reduce-scatter.19.cloned.1.call-start = ((), (), s32[]{:S(2)}) async-start(), calls=%async_computation.14 | async-start | bytes 884736 | tf_op jit(solution)/shard_map/reduce_scatter | solution.py:258
  425.9 359.0 %reduce-scatter.23.cloned.1.call-start = ((), (), s32[]{:S(2)}) async-start(), calls=%async_computation.16 | async-start | bytes 2654208 | tf_op jit(solution)/shard_map/reduce_scatter | solution.py:262
  430.7 427.0 %reduce-scatter.21.cloned.1.call-start = ((), (), s32[]{:S(2)}) async-start(), calls=%async_computation.15 | async-start | bytes 2654208 | tf_op jit(solution)/shard_map/reduce_scatter | solution.py:261
  436.1 494.5 %reduce-scatter.17.cloned.1.call-start = ((), (), s32[]{:S(2)}) async-start(), calls=%async_computation.13 | async-start | bytes 2654208 | tf_op jit(solution)/shard_map/reduce_scatter | solution.py:256
  440.9 549.9 %reduce-scatter.15.cloned.1.call-start = ((), (), s32[]{:S(2)}) async-start(), calls=%async_computation.12 | async-start | bytes 7864320 | tf_op jit(solution)/shard_map/reduce_scatter | solution.py:203
  448.7 15.1 %copy-start.36 = (f32[1024]{0:T(1024)S(1)}, f32[1024]{0:T(1024)}, u32[]{:S(2)}) copy-start(f32[1024]{0:T(1024)} %copy-done.35) | copy-start | bytes 12292
  448.7 15.1 %copy-start.38 = (f32[1024]{0:T(1024)S(1)}, f32[1024]{0:T(1024)}, u32[]{:S(2)}) copy-start(f32[1024]{0:T(1024)} %copy-done.37) | copy-start | bytes 12292
  448.7 15.1 %copy-start.41 = (f32[768]{0:T(1024)S(1)}, f32[768]{0:T(1024)}, u32[]{:S(2)}) copy-start(f32[768]{0:T(1024)} %param.24) | copy-start | bytes 9220
  448.7 17.9 %copy-start.50 = (f32[768]{0:T(1024)S(1)}, f32[768]{0:T(1024)}, u32[]{:S(2)}) copy-start(f32[768]{0:T(1024)} %get-tuple-element.107) | copy-start | bytes 9220
  448.7 17.9 %copy-start.53 = (f32[768]{0:T(1024)S(1)}, f32[768]{0:T(1024)}, u32[]{:S(2)}) copy-start(f32[768]{0:T(1024)} %get-tuple-element.82) | copy-start | bytes 9220
  448.7 17.9 %copy-start.54 = (f32[768]{0:T(1024)S(1)}, f32[768]{0:T(1024)}, u32[]{:S(2)}) copy-start(f32[768]{0:T(1024)} %get-tuple-element.89) | copy-start | bytes 9220
  448.7 17.9 %copy-start.55 = (f32[768]{0:T(1024)S(1)}, f32[768]{0:T(1024)}, u32[]{:S(2)}) copy-start(f32[768]{0:T(1024)} %get-tuple-element.80) | copy-start | bytes 9220
  448.7 17.9 %copy-start.56 = (f32[768]{0:T(1024)S(1)}, f32[768]{0:T(1024)}, u32[]{:S(2)}) copy-start(f32[768]{0:T(1024)} %get-tuple-element.90) | copy-start | bytes 9220
  448.7 17.9 %copy-start.61 = (f32[768]{0:T(1024)S(1)}, f32[768]{0:T(1024)}, u32[]{:S(2)}) copy-start(f32[768]{0:T(1024)} %get-tuple-element.102) | copy-start | bytes 9220
  (55 other events, 164.1 us)
Sparse Core Ops, SparseCore 0:
  43.2 49.0 all-gather.9
  93.9 46.3 all-gather.7
  158.4 46.3 all-gather.11
  238.6 42.8 all-reduce.4
  309.3 42.8 all-reduce.6
  355.4 63.3 reduce-scatter.28
  421.7 41.9 all-reduce.8
  467.0 63.3 reduce-scatter.24
  533.8 63.8 reduce-scatter.26
  599.7 45.3 all-gather.13
  649.0 63.1 reduce-scatter.18
  716.2 68.6 reduce-scatter.22
  788.9 68.7 reduce-scatter.20
  861.6 68.9 reduce-scatter.16
  933.5 57.1 reduce-scatter.14
